TPU v7x, 128 devices: a whole 4x4x4 slice. The times are simulated.
128 devices in a mesh: shot: 4 (over y_lo, core), gx: 4 (over z), gy: 8 (over x, y_hi).
Axes of the slice: x: 4, y: 4 (y_hi: 2, y_lo: 2; y = y_hi * 2 + y_lo), z: 4, core: 2. Of those that a mesh axis runs over, the one named last changes fastest.
Arguments:
- model_tiles: float32 [256, 256, 128], P(('shot', 'gx'), 'gy'), may hold values from 0.2 to 0.45
- owner_map: int32 [16], replicated, may hold values from 0 to 15, each once
- offsets: int32 [4], P('shot'), may hold values from 0 to 12
- field_now: float32 [4, 2, 64, 256, 128], P('shot', None, 'gx', 'gy'), may hold values from -6 to 6
- field_prev: float32 [4, 2, 64, 256, 128], P('shot', None, 'gx', 'gy'), may hold values from -6 to 6
- sources: int32 [4, 2, 3], P('shot'), may hold values from 0 to 255, as said below
- wavelet: float32 [4, 2, 8], P('shot'), may hold values from -6 to 6
- receivers: int32 [4, 256, 3], P('shot'), may hold values from 0 to 255, as said below
Outputs:
- out_now: float32 [4, 2, 64, 256, 128], P('shot', None, 'gx', 'gy')
- out_prev: float32 [4, 2, 64, 256, 128], P('shot', None, 'gx', 'gy')
- traces: float32 [4, 2, 256, 8], P('shot')
Inputs may be any that keep to these rules, and one draw needn't show every extreme that they name: `sources`: each row is a cell of the group's aperture: first entry below 64, second below 256, third below 128. `receivers`: each row is a cell of the group's aperture: first entry below 64, second below 256, third below 128.
All inputs are finite; a program needn't handle non-finite values.
Results may differ from a plain program's by a relative error of at most 0.0003.
Values sent between devices are 32-bit elements; how exact they have to be, the bound alone decides.
A program may use at most 128 MiB of HBM per device.

v0:
```python
import jax
import jax.numpy as jnp
from jax import lax
from jax.sharding import PartitionSpec as P

STEPS = 8
center_weight = -2.5
near_weight = 4.0 / 3.0
far_weight = -1.0 / 12.0
damp_peak = 0.3


def extended_2(cells, sides, width):
    for axis, dim in sides:
        count = lax.axis_size(axis)
        ends = count - 1
        head = lax.slice_in_dim(cells, 0, width, axis=dim)
        tail = lax.slice_in_dim(cells, cells.shape[dim] - width, cells.shape[dim], axis=dim)
        cells = jnp.concatenate(
            [
                lax.ppermute(tail, axis, [(i, (i + 1) % count) for i in range(ends)]),
                cells,
                lax.ppermute(head, axis, [((i + 1) % count, i) for i in range(ends)]),
            ],
            axis=dim,
        )
    return cells


def depth_ahead(field, reach):
    filler = jnp.zeros(field.shape[:-1] + (reach,), field.dtype)
    return jnp.concatenate([field[..., reach:], filler], axis=-1)


def depth_behind(field, reach):
    filler = jnp.zeros(field.shape[:-1] + (reach,), field.dtype)
    return jnp.concatenate([filler, field[..., :-reach]], axis=-1)


def laplace(extended):
    middle = extended[:, 2:-2, 2:-2]
    along_x = (
        center_weight * middle
        + near_weight * (extended[:, 3:-1, 2:-2] + extended[:, 1:-3, 2:-2])
        + far_weight * (extended[:, 4:, 2:-2] + extended[:, :-4, 2:-2])
    )
    along_y = (
        center_weight * middle
        + near_weight * (extended[:, 2:-2, 3:-1] + extended[:, 2:-2, 1:-3])
        + far_weight * (extended[:, 2:-2, 4:] + extended[:, 2:-2, :-4])
    )
    along_z = (
        center_weight * middle
        + near_weight * (depth_ahead(middle, 1) + depth_behind(middle, 1))
        + far_weight * (depth_ahead(middle, 2) + depth_behind(middle, 2))
    )
    return along_x + along_y + along_z


def damping(x_cells, y_cells, width, x_total, y_total):
    x_depth = (
        jnp.maximum(width - jnp.minimum(x_cells + 1, x_total - x_cells), 0).astype(jnp.float32)
        / width
    )
    y_depth = (
        jnp.maximum(width - jnp.minimum(y_cells + 1, y_total - y_cells), 0).astype(jnp.float32)
        / width
    )
    return damp_peak * (x_depth[:, None] * x_depth[:, None] + y_depth[None, :] * y_depth[None, :])


def injection(x_cells, y_cells, z_cells, source_cells, amplitude):
    on_x = (x_cells[None, :] == source_cells[:, 0:1]).astype(jnp.float32)
    on_y = (y_cells[None, :] == source_cells[:, 1:2]).astype(jnp.float32)
    on_z = (z_cells[None, :] == source_cells[:, 2:3]).astype(jnp.float32)
    return (
        amplitude[:, None, None, None]
        * on_x[:, :, None, None]
        * on_y[:, None, :, None]
        * on_z[:, None, None, :]
    )


def advance(extended, previous, coef, damp, inject):
    middle = extended[:, 2:-2, 2:-2]
    return (2.0 * middle - (1.0 - damp) * previous + coef * laplace(extended) + inject) / (
        1.0 + damp
    )


def sample(field, receiver_cells, x_start, y_start):
    size_x, size_y = (field.shape[1], field.shape[2])
    local_x = receiver_cells[:, 0] - x_start
    local_y = receiver_cells[:, 1] - y_start
    inside = (local_x >= 0) & (local_x < size_x) & (local_y >= 0) & (local_y < size_y)
    values = field[
        :, jnp.clip(local_x, 0, size_x - 1), jnp.clip(local_y, 0, size_y - 1), receiver_cells[:, 2]
    ]
    return jnp.where(inside[None, :], values, 0.0)


def local(model_tiles, owner_map, offsets, field_now, field_prev, sources, wavelet, receivers):
    block_x, block_y, depth = model_tiles.shape
    column_index = lax.axis_index("gx")
    row_index = lax.axis_index("gy")
    across = lax.axis_size("gx")
    total_x = block_x * across
    total_y = block_y * lax.axis_size("gy")
    shift_x = offsets[0]
    tile_total = owner_map.shape[0]
    column_ids = jnp.arange(tile_total, dtype=jnp.int32)
    wanted = jnp.sum(jnp.where(column_ids == shift_x + column_index, owner_map, 0))
    piece = lax.all_gather(model_tiles, ("shot", "gx"), axis=0, tiled=True)
    rows = wanted * block_x + jnp.arange(block_x, dtype=jnp.int32)
    inside = (rows >= 0) & (rows < piece.shape[0])
    taken = jnp.take(piece, jnp.clip(rows, 0, piece.shape[0] - 1), axis=0)
    speed = jnp.where(inside[:, None, None], taken, jnp.zeros_like(model_tiles))
    coef = speed * speed
    current = field_now[0]
    previous = field_prev[0]
    source_cells = sources[0]
    amplitudes = wavelet[0]
    receiver_cells = receivers[0]
    x_start = column_index * block_x
    y_start = row_index * block_y
    x_here = x_start + jnp.arange(block_x, dtype=jnp.int32)
    y_here = y_start + jnp.arange(block_y, dtype=jnp.int32)
    z_cells = jnp.arange(depth, dtype=jnp.int32)
    damp = damping(x_here, y_here, block_x, total_x, total_y)[:, :, None]
    recorded = []
    for step in range(STEPS):
        extended = extended_2(current, (("gx", 1), ("gy", 2)), 2)
        inject = injection(x_here, y_here, z_cells, source_cells, amplitudes[:, step])
        fresh = advance(extended, previous, coef, damp, inject)
        recorded.append(sample(fresh, receiver_cells, x_start, y_start))
        previous = current
        current = fresh
    traces = lax.psum(jnp.stack(recorded, axis=-1), ("gx", "gy"))
    return (current[None], previous[None], traces[None])


def solution(mesh):
    return jax.shard_map(
        local,
        mesh=mesh,
        in_specs=(
            P(("shot", "gx"), "gy", None),
            P(),
            P("shot"),
            P("shot", None, "gx", "gy", None),
            P("shot", None, "gx", "gy", None),
            P("shot", None, None),
            P("shot", None, None),
            P("shot", None, None),
        ),
        out_specs=(
            P("shot", None, "gx", "gy", None),
            P("shot", None, "gx", "gy", None),
            P("shot", None, None, None),
        ),
        check_vma=False,
    )
```

profile of v0, /device:TPU:0, one launch (start us, length us, event | category | flops | bytes accessed | tf_op | source)
XLA Modules:
  0.0 552.9 jit_solution(16876477504030605119)
XLA Ops:
  28.2 6.1 %collective-permute-start.3 = (f32[2,20,2,128]{3,2,1,0:T(2,128)S(1)}, f32[2,20,2,128]{3,2,1,0:T(2,128)S(1)}, u32[]{:S(2)}, u32[]{:S(2)}) collective-permute-start(f32[2,20,2,128]{3,2,1,0:T(2,128)S(1)} %get-tuple-element.57), channel_id=1, source_target_pairs={{0,1},{1,2},{2,3},{3,4},{4,5},{5,6},{6,7},{8,9},{9,10},{10,11},{11... | collective-permute-start | bytes 122888 | tf_op jit(solution)/shard_map/ppermute | solution.py:21
  37.5 24.6 %all-gather.2.cloned.1.call-done = f32[256,32,128]{2,1,0:T(8,128)} async-done(((f32[16,32,128]{2,1,0:T(8,128)}), f32[256,32,128]{2,1,0:T(8,128)}) %all-gather.2.cloned.1.call-update) | async-done | bytes 4194320 | tf_op jit(solution)/shard_map/all_gather | solution.py:113
  77.4 6.1 %collective-permute-start.7 = (f32[2,20,2,128]{3,2,1,0:T(2,128)S(1)}, f32[2,20,2,128]{3,2,1,0:T(2,128)S(1)}, u32[]{:S(2)}, u32[]{:S(2)}) collective-permute-start(f32[2,20,2,128]{3,2,1,0:T(2,128)S(1)} %get-tuple-element.53), channel_id=1, source_target_pairs={{0,1},{1,2},{2,3},{3,4},{4,5},{5,6},{6,7},{8,9},{9,10},{10,11},{11... | collective-permute-start | bytes 122888 | tf_op jit(solution)/shard_map/ppermute | solution.py:21
  84.4 16.7 %copy.515 = f32[2,16,32,128]{0,3,2,1:T(8,128)} copy(f32[2,16,32,128]{3,2,1,0:T(8,128)S(1)} %fusion.94) | data formatting | bytes 1048576 | tf_op jit(solution)/shard_map/div | solution.py:86
  107.5 5.0 collective-permute-start.9
  115.8 6.5 %collective-permute-start.11 = (f32[2,20,2,128]{3,2,1,0:T(2,128)S(1)}, f32[2,20,2,128]{3,2,1,0:T(2,128)S(1)}, u32[]{:S(2)}, u32[]{:S(2)}) collective-permute-start(f32[2,20,2,128]{3,2,1,0:T(2,128)S(1)} %get-tuple-element.49), channel_id=1, source_target_pairs={{0,1},{1,2},{2,3},{3,4},{4,5},{5,6},{6,7},{8,9},{9,10},{10,11},{11... | collective-permute-start | bytes 122888 | tf_op jit(solution)/shard_map/ppermute | solution.py:21
  123.2 16.7 %copy.516 = f32[2,16,32,128]{0,3,2,1:T(8,128)} copy(f32[2,16,32,128]{3,2,1,0:T(8,128)S(1)} %fusion.82) | data formatting | bytes 1048576 | tf_op jit(solution)/shard_map/div | solution.py:86
  146.4 4.9 collective-permute-start.13
  154.5 6.9 %collective-permute-start.15 = (f32[2,20,2,128]{3,2,1,0:T(2,128)S(1)}, f32[2,20,2,128]{3,2,1,0:T(2,128)S(1)}, u32[]{:S(2)}, u32[]{:S(2)}) collective-permute-start(f32[2,20,2,128]{3,2,1,0:T(2,128)S(1)} %get-tuple-element.45), channel_id=1, source_target_pairs={{0,1},{1,2},{2,3},{3,4},{4,5},{5,6},{6,7},{8,9},{9,10},{10,11},{11... | collective-permute-start | bytes 122888 | tf_op jit(solution)/shard_map/ppermute | solution.py:21
  162.4 16.7 %copy.517 = f32[2,16,32,128]{0,3,2,1:T(8,128)} copy(f32[2,16,32,128]{3,2,1,0:T(8,128)S(1)} %fusion.70) | data formatting | bytes 1048576 | tf_op jit(solution)/shard_map/div | solution.py:86
  185.6 4.9 collective-permute-start.17
  193.7 7.1 %collective-permute-start.19 = (f32[2,20,2,128]{3,2,1,0:T(2,128)S(1)}, f32[2,20,2,128]{3,2,1,0:T(2,128)S(1)}, u32[]{:S(2)}, u32[]{:S(2)}) collective-permute-start(f32[2,20,2,128]{3,2,1,0:T(2,128)S(1)} %get-tuple-element.41), channel_id=1, source_target_pairs={{0,1},{1,2},{2,3},{3,4},{4,5},{5,6},{6,7},{8,9},{9,10},{10,11},{11... | collective-permute-start | bytes 122888 | tf_op jit(solution)/shard_map/ppermute | solution.py:21
  201.7 16.7 %copy.518 = f32[2,16,32,128]{0,3,2,1:T(8,128)} copy(f32[2,16,32,128]{3,2,1,0:T(8,128)S(1)} %fusion.58) | data formatting | bytes 1048576 | tf_op jit(solution)/shard_map/div | solution.py:86
  224.9 4.9 collective-permute-start.21
  233.0 6.9 %collective-permute-start.23 = (f32[2,20,2,128]{3,2,1,0:T(2,128)S(1)}, f32[2,20,2,128]{3,2,1,0:T(2,128)S(1)}, u32[]{:S(2)}, u32[]{:S(2)}) collective-permute-start(f32[2,20,2,128]{3,2,1,0:T(2,128)S(1)} %get-tuple-element.37), channel_id=1, source_target_pairs={{0,1},{1,2},{2,3},{3,4},{4,5},{5,6},{6,7},{8,9},{9,10},{10,11},{11... | collective-permute-start | bytes 122888 | tf_op jit(solution)/shard_map/ppermute | solution.py:21
  240.9 16.7 %copy.519 = f32[2,16,32,128]{0,3,2,1:T(8,128)} copy(f32[2,16,32,128]{3,2,1,0:T(8,128)S(1)} %fusion.46) | data formatting | bytes 1048576 | tf_op jit(solution)/shard_map/div | solution.py:86
  264.1 4.9 collective-permute-start.25
  272.2 6.9 %collective-permute-start.27 = (f32[2,20,2,128]{3,2,1,0:T(2,128)S(1)}, f32[2,20,2,128]{3,2,1,0:T(2,128)S(1)}, u32[]{:S(2)}, u32[]{:S(2)}) collective-permute-start(f32[2,20,2,128]{3,2,1,0:T(2,128)S(1)} %get-tuple-element.33), channel_id=1, source_target_pairs={{0,1},{1,2},{2,3},{3,4},{4,5},{5,6},{6,7},{8,9},{9,10},{10,11},{11... | collective-permute-start | bytes 122888 | tf_op jit(solution)/shard_map/ppermute | solution.py:21
  280.1 16.7 %copy.520 = f32[2,16,32,128]{0,3,2,1:T(8,128)} copy(f32[2,16,32,128]{3,2,1,0:T(8,128)S(1)} %fusion.34) | data formatting | bytes 1048576 | tf_op jit(solution)/shard_map/div | solution.py:86
  303.2 4.9 collective-permute-start.29
  311.3 7.2 %collective-permute-start.31 = (f32[2,20,2,128]{3,2,1,0:T(2,128)S(1)}, f32[2,20,2,128]{3,2,1,0:T(2,128)S(1)}, u32[]{:S(2)}, u32[]{:S(2)}) collective-permute-start(f32[2,20,2,128]{3,2,1,0:T(2,128)S(1)} %get-tuple-element.29), channel_id=1, source_target_pairs={{0,1},{1,2},{2,3},{3,4},{4,5},{5,6},{6,7},{8,9},{9,10},{10,11},{11... | collective-permute-start | bytes 122888 | tf_op jit(solution)/shard_map/ppermute | solution.py:21
  319.5 16.7 %copy.521 = f32[2,16,32,128]{0,3,2,1:T(8,128)} copy(f32[2,16,32,128]{3,2,1,0:T(8,128)S(1)} %fusion.22) | data formatting | bytes 1048576 | tf_op jit(solution)/shard_map/div | solution.py:86
  341.3 16.8 %copy.522 = f32[2,16,32,128]{0,3,2,1:T(8,128)} copy(f32[2,16,32,128]{3,2,1,0:T(8,128)S(1)} %fusion.10) | data formatting | bytes 1048576 | tf_op jit(solution)/shard_map/div | solution.py:86
  362.6 183.4 %psum.7 = f32[1,2,256,8]{2,3,1,0:T(8,128)} all-reduce(f32[1,2,256,8]{2,3,1,0:T(8,128)S(1)} %bitcast.70), channel_id=1, replica_groups=mesh['shot'=4,'gx'=4,'gy'=8] {'gx','gy'}, use_global_device_ids=true, to_apply=%region_1.2 | all-reduce | flops 4096 | bytes 32768 | tf_op jit(solution)/shard_map/psum | solution.py:138
  (164 shorter events, 112.2 us)
Async XLA Ops:
  7.2 54.9 %all-gather.2.cloned.1.call-start = ((), (), s32[]{:S(2)}) async-start(), calls=%async_computation | async-start | bytes 4456448 | tf_op jit(solution)/shard_map/all_gather | solution.py:113
  8.8 17.0 %collective-permute-start = (f32[2,2,32,128]{3,2,1,0:T(8,128)S(1)}, f32[2,2,32,128]{3,2,1,0:T(8,128)S(1)}, u32[]{:S(2)}, u32[]{:S(2)}) collective-permute-start(f32[2,2,32,128]{3,2,1,0:T(8,128)S(1)} %get-tuple-element.104), channel_id=1, source_target_pairs={{8,0},{16,8},{24,16},{9,1},{17,9},{25,17},{10,2},{18,10},{26,18},{... | collective-permute-start | bytes 196616 | tf_op jit(solution)/shard_map/ppermute | solution.py:23
  10.1 15.8 %collective-permute-start.1 = (f32[2,2,32,128]{3,2,1,0:T(8,128)S(1)}, f32[2,2,32,128]{3,2,1,0:T(8,128)S(1)}, u32[]{:S(2)}, u32[]{:S(2)}) collective-permute-start(f32[2,2,32,128]{3,2,1,0:T(8,128)S(1)} %get-tuple-element.105), channel_id=1, source_target_pairs={{0,8},{8,16},{16,24},{1,9},{9,17},{17,25},{2,10},{10,18},{18,26},{... | collective-permute-start | bytes 196616 | tf_op jit(solution)/shard_map/ppermute | solution.py:21
  26.9 7.7 %collective-permute-start.2 = (f32[2,20,2,128]{3,2,1,0:T(2,128)S(1)}, f32[2,20,2,128]{3,2,1,0:T(2,128)S(1)}, u32[]{:S(2)}, u32[]{:S(2)}) collective-permute-start(f32[2,20,2,128]{3,2,1,0:T(2,128)S(1)} %get-tuple-element.56), channel_id=1, source_target_pairs={{1,0},{2,1},{3,2},{4,3},{5,4},{6,5},{7,6},{9,8},{10,9},{11,10},{12... | collective-permute-start | bytes 122888 | tf_op jit(solution)/shard_map/ppermute | solution.py:23
  28.2 7.9 %collective-permute-start.3 = (f32[2,20,2,128]{3,2,1,0:T(2,128)S(1)}, f32[2,20,2,128]{3,2,1,0:T(2,128)S(1)}, u32[]{:S(2)}, u32[]{:S(2)}) collective-permute-start(f32[2,20,2,128]{3,2,1,0:T(2,128)S(1)} %get-tuple-element.57), channel_id=1, source_target_pairs={{0,1},{1,2},{2,3},{3,4},{4,5},{5,6},{6,7},{8,9},{9,10},{10,11},{11... | collective-permute-start | bytes 122888 | tf_op jit(solution)/shard_map/ppermute | solution.py:21
  68.1 6.8 %collective-permute-start.4 = (f32[2,2,32,128]{3,2,1,0:T(8,128)S(1)}, f32[2,2,32,128]{3,2,1,0:T(8,128)S(1)}, u32[]{:S(2)}, u32[]{:S(2)}) collective-permute-start(f32[2,2,32,128]{3,2,1,0:T(8,128)S(1)} %get-tuple-element.98), channel_id=1, source_target_pairs={{8,0},{16,8},{24,16},{9,1},{17,9},{25,17},{10,2},{18,10},{26,18},{... | collective-permute-start | bytes 196616 | tf_op jit(solution)/shard_map/ppermute | solution.py:23
  76.1 28.0 %collective-permute-start.6 = (f32[2,20,2,128]{3,2,1,0:T(2,128)S(1)}, f32[2,20,2,128]{3,2,1,0:T(2,128)S(1)}, u32[]{:S(2)}, u32[]{:S(2)}) collective-permute-start(f32[2,20,2,128]{3,2,1,0:T(2,128)S(1)} %get-tuple-element.52), channel_id=1, source_target_pairs={{1,0},{2,1},{3,2},{4,3},{5,4},{6,5},{7,6},{9,8},{10,9},{11,10},{12... | collective-permute-start | bytes 122888 | tf_op jit(solution)/shard_map/ppermute | solution.py:23
  77.4 26.7 %collective-permute-start.7 = (f32[2,20,2,128]{3,2,1,0:T(2,128)S(1)}, f32[2,20,2,128]{3,2,1,0:T(2,128)S(1)}, u32[]{:S(2)}, u32[]{:S(2)}) collective-permute-start(f32[2,20,2,128]{3,2,1,0:T(2,128)S(1)} %get-tuple-element.53), channel_id=1, source_target_pairs={{0,1},{1,2},{2,3},{3,4},{4,5},{5,6},{6,7},{8,9},{9,10},{10,11},{11... | collective-permute-start | bytes 122888 | tf_op jit(solution)/shard_map/ppermute | solution.py:21
  107.5 6.9 %collective-permute-start.9 = (f32[2,2,32,128]{3,2,1,0:T(8,128)S(1)}, f32[2,2,32,128]{3,2,1,0:T(8,128)S(1)}, u32[]{:S(2)}, u32[]{:S(2)}) collective-permute-start(f32[2,2,32,128]{3,2,1,0:T(8,128)S(1)} %get-tuple-element.93), channel_id=1, source_target_pairs={{0,8},{8,16},{16,24},{1,9},{9,17},{17,25},{2,10},{10,18},{18,26},{... | collective-permute-start | bytes 196616 | tf_op jit(solution)/shard_map/ppermute | solution.py:21
  114.5 28.5 %collective-permute-start.10 = (f32[2,20,2,128]{3,2,1,0:T(2,128)S(1)}, f32[2,20,2,128]{3,2,1,0:T(2,128)S(1)}, u32[]{:S(2)}, u32[]{:S(2)}) collective-permute-start(f32[2,20,2,128]{3,2,1,0:T(2,128)S(1)} %get-tuple-element.48), channel_id=1, source_target_pairs={{1,0},{2,1},{3,2},{4,3},{5,4},{6,5},{7,6},{9,8},{10,9},{11,10},{12... | collective-permute-start | bytes 122888 | tf_op jit(solution)/shard_map/ppermute | solution.py:23
  115.8 27.2 %collective-permute-start.11 = (f32[2,20,2,128]{3,2,1,0:T(2,128)S(1)}, f32[2,20,2,128]{3,2,1,0:T(2,128)S(1)}, u32[]{:S(2)}, u32[]{:S(2)}) collective-permute-start(f32[2,20,2,128]{3,2,1,0:T(2,128)S(1)} %get-tuple-element.49), channel_id=1, source_target_pairs={{0,1},{1,2},{2,3},{3,4},{4,5},{5,6},{6,7},{8,9},{9,10},{10,11},{11... | collective-permute-start | bytes 122888 | tf_op jit(solution)/shard_map/ppermute | solution.py:21
  146.4 6.8 %collective-permute-start.13 = (f32[2,2,32,128]{3,2,1,0:T(8,128)S(1)}, f32[2,2,32,128]{3,2,1,0:T(8,128)S(1)}, u32[]{:S(2)}, u32[]{:S(2)}) collective-permute-start(f32[2,2,32,128]{3,2,1,0:T(8,128)S(1)} %get-tuple-element.87), channel_id=1, source_target_pairs={{0,8},{8,16},{16,24},{1,9},{9,17},{17,25},{2,10},{10,18},{18,26},{... | collective-permute-start | bytes 196616 | tf_op jit(solution)/shard_map/ppermute | solution.py:21
  153.2 28.9 %collective-permute-start.14 = (f32[2,20,2,128]{3,2,1,0:T(2,128)S(1)}, f32[2,20,2,128]{3,2,1,0:T(2,128)S(1)}, u32[]{:S(2)}, u32[]{:S(2)}) collective-permute-start(f32[2,20,2,128]{3,2,1,0:T(2,128)S(1)} %get-tuple-element.44), channel_id=1, source_target_pairs={{1,0},{2,1},{3,2},{4,3},{5,4},{6,5},{7,6},{9,8},{10,9},{11,10},{12... | collective-permute-start | bytes 122888 | tf_op jit(solution)/shard_map/ppermute | solution.py:23
  154.5 27.6 %collective-permute-start.15 = (f32[2,20,2,128]{3,2,1,0:T(2,128)S(1)}, f32[2,20,2,128]{3,2,1,0:T(2,128)S(1)}, u32[]{:S(2)}, u32[]{:S(2)}) collective-permute-start(f32[2,20,2,128]{3,2,1,0:T(2,128)S(1)} %get-tuple-element.45), channel_id=1, source_target_pairs={{0,1},{1,2},{2,3},{3,4},{4,5},{5,6},{6,7},{8,9},{9,10},{10,11},{11... | collective-permute-start | bytes 122888 | tf_op jit(solution)/shard_map/ppermute | solution.py:21
  185.6 6.8 %collective-permute-start.17 = (f32[2,2,32,128]{3,2,1,0:T(8,128)S(1)}, f32[2,2,32,128]{3,2,1,0:T(8,128)S(1)}, u32[]{:S(2)}, u32[]{:S(2)}) collective-permute-start(f32[2,2,32,128]{3,2,1,0:T(8,128)S(1)} %get-tuple-element.81), channel_id=1, source_target_pairs={{0,8},{8,16},{16,24},{1,9},{9,17},{17,25},{2,10},{10,18},{18,26},{... | collective-permute-start | bytes 196616 | tf_op jit(solution)/shard_map/ppermute | solution.py:21
  192.4 29.1 %collective-permute-start.18 = (f32[2,20,2,128]{3,2,1,0:T(2,128)S(1)}, f32[2,20,2,128]{3,2,1,0:T(2,128)S(1)}, u32[]{:S(2)}, u32[]{:S(2)}) collective-permute-start(f32[2,20,2,128]{3,2,1,0:T(2,128)S(1)} %get-tuple-element.40), channel_id=1, source_target_pairs={{1,0},{2,1},{3,2},{4,3},{5,4},{6,5},{7,6},{9,8},{10,9},{11,10},{12... | collective-permute-start | bytes 122888 | tf_op jit(solution)/shard_map/ppermute | solution.py:23
  193.7 27.8 %collective-permute-start.19 = (f32[2,20,2,128]{3,2,1,0:T(2,128)S(1)}, f32[2,20,2,128]{3,2,1,0:T(2,128)S(1)}, u32[]{:S(2)}, u32[]{:S(2)}) collective-permute-start(f32[2,20,2,128]{3,2,1,0:T(2,128)S(1)} %get-tuple-element.41), channel_id=1, source_target_pairs={{0,1},{1,2},{2,3},{3,4},{4,5},{5,6},{6,7},{8,9},{9,10},{10,11},{11... | collective-permute-start | bytes 122888 | tf_op jit(solution)/shard_map/ppermute | solution.py:21
  231.7 28.9 %collective-permute-start.22 = (f32[2,20,2,128]{3,2,1,0:T(2,128)S(1)}, f32[2,20,2,128]{3,2,1,0:T(2,128)S(1)}, u32[]{:S(2)}, u32[]{:S(2)}) collective-permute-start(f32[2,20,2,128]{3,2,1,0:T(2,128)S(1)} %get-tuple-element.36), channel_id=1, source_target_pairs={{1,0},{2,1},{3,2},{4,3},{5,4},{6,5},{7,6},{9,8},{10,9},{11,10},{12... | collective-permute-start | bytes 122888 | tf_op jit(solution)/shard_map/ppermute | solution.py:23
  233.0 27.6 %collective-permute-start.23 = (f32[2,20,2,128]{3,2,1,0:T(2,128)S(1)}, f32[2,20,2,128]{3,2,1,0:T(2,128)S(1)}, u32[]{:S(2)}, u32[]{:S(2)}) collective-permute-start(f32[2,20,2,128]{3,2,1,0:T(2,128)S(1)} %get-tuple-element.37), channel_id=1, source_target_pairs={{0,1},{1,2},{2,3},{3,4},{4,5},{5,6},{6,7},{8,9},{9,10},{10,11},{11... | collective-permute-start | bytes 122888 | tf_op jit(solution)/shard_map/ppermute | solution.py:21
  264.1 6.8 %collective-permute-start.25 = (f32[2,2,32,128]{3,2,1,0:T(8,128)S(1)}, f32[2,2,32,128]{3,2,1,0:T(8,128)S(1)}, u32[]{:S(2)}, u32[]{:S(2)}) collective-permute-start(f32[2,2,32,128]{3,2,1,0:T(8,128)S(1)} %get-tuple-element.69), channel_id=1, source_target_pairs={{0,8},{8,16},{16,24},{1,9},{9,17},{17,25},{2,10},{10,18},{18,26},{... | collective-permute-start | bytes 196616 | tf_op jit(solution)/shard_map/ppermute | solution.py:21
  270.9 28.9 %collective-permute-start.26 = (f32[2,20,2,128]{3,2,1,0:T(2,128)S(1)}, f32[2,20,2,128]{3,2,1,0:T(2,128)S(1)}, u32[]{:S(2)}, u32[]{:S(2)}) collective-permute-start(f32[2,20,2,128]{3,2,1,0:T(2,128)S(1)} %get-tuple-element.32), channel_id=1, source_target_pairs={{1,0},{2,1},{3,2},{4,3},{5,4},{6,5},{7,6},{9,8},{10,9},{11,10},{12... | collective-permute-start | bytes 122888 | tf_op jit(solution)/shard_map/ppermute | solution.py:23
  272.2 27.6 %collective-permute-start.27 = (f32[2,20,2,128]{3,2,1,0:T(2,128)S(1)}, f32[2,20,2,128]{3,2,1,0:T(2,128)S(1)}, u32[]{:S(2)}, u32[]{:S(2)}) collective-permute-start(f32[2,20,2,128]{3,2,1,0:T(2,128)S(1)} %get-tuple-element.33), channel_id=1, source_target_pairs={{0,1},{1,2},{2,3},{3,4},{4,5},{5,6},{6,7},{8,9},{9,10},{10,11},{11... | collective-permute-start | bytes 122888 | tf_op jit(solution)/shard_map/ppermute | solution.py:21
  310.0 29.1 %collective-permute-start.30 = (f32[2,20,2,128]{3,2,1,0:T(2,128)S(1)}, f32[2,20,2,128]{3,2,1,0:T(2,128)S(1)}, u32[]{:S(2)}, u32[]{:S(2)}) collective-permute-start(f32[2,20,2,128]{3,2,1,0:T(2,128)S(1)} %get-tuple-element.28), channel_id=1, source_target_pairs={{1,0},{2,1},{3,2},{4,3},{5,4},{6,5},{7,6},{9,8},{10,9},{11,10},{12... | collective-permute-start | bytes 122888 | tf_op jit(solution)/shard_map/ppermute | solution.py:23
  311.3 27.8 %collective-permute-start.31 = (f32[2,20,2,128]{3,2,1,0:T(2,128)S(1)}, f32[2,20,2,128]{3,2,1,0:T(2,128)S(1)}, u32[]{:S(2)}, u32[]{:S(2)}) collective-permute-start(f32[2,20,2,128]{3,2,1,0:T(2,128)S(1)} %get-tuple-element.29), channel_id=1, source_target_pairs={{0,1},{1,2},{2,3},{3,4},{4,5},{5,6},{6,7},{8,9},{9,10},{10,11},{11... | collective-permute-start | bytes 122888 | tf_op jit(solution)/shard_map/ppermute | solution.py:21
  (22 other events, 717.0 us)
Sparse Core Ops, SparseCore 0:
  9.7 52.3 all-gather.1
where the time goes:
time: 554 us; the launch traced here: 553 us
  blocking collectives  183 us (33%)
  local copies, waits for them, and re-layouts  177 us (32%)
  starting transfers between devices  113 us (20%)
  waiting for transfers between devices  39.1 us (7%)
  other arithmetic  24.3 us (4%)
  between operations  16 us (3%)
    psum x1, blocking collectives, local(): traces = lax.psum(jnp.stack(recorded, axis=-1), ('gx', 'gy'))  183 us
    div x8, local copies, waits for them, and re-layouts, advance(): (2.0 * middle - (1.0 - damp) * previous + coef * laplace(extended) + inje...  134 us
    ppermute x16, starting transfers between devices, extended_2(): lax.ppermute(tail, axis, [(i, (i + 1) % count) for i in range(ends)])  92.2 us
    all_gather x1, waiting for transfers between devices, local(): piece = lax.all_gather(model_tiles, ('shot', 'gx'), axis=0, tiled=True)  24.6 us
    gather x8, local copies, waits for them, and re-layouts, sample(): field[:, jnp.clip(local_x, 0, size_x - 1), jnp.clip(local_y, 0, size_y -...  23.6 us
    ppermute x16, starting transfers between devices, extended_2(): lax.ppermute(head, axis, [((i + 1) % count, i) for i in range(ends)])  20.7 us
    div x8, other arithmetic, advance(): (2.0 * middle - (1.0 - damp) * previous + coef * laplace(extended) + inje...  16.9 us
    slice x16, local copies, waits for them, and re-layouts, depth_ahead(): return jnp.concatenate([field[..., reach:], filler], axis=-1)  12.5 us
  transfers between devices with their start and end apart: 33, of which 17 were waited for; matrix products, arithmetic and copies ran while one was open for 29% of the time, Pallas kernels for 0%

commit v1 on v0

--- a/solution.py
+++ b/solution.py
@@ -135,7 +135,7 @@
         recorded.append(sample(fresh, receiver_cells, x_start, y_start))
         previous = current
         current = fresh
-    traces = lax.psum(jnp.stack(recorded, axis=-1), ("gx", "gy"))
+    traces = lax.psum(lax.psum(jnp.stack(recorded, axis=-1), "gy"), "gx")
     return (current[None], previous[None], traces[None])
 
 

time: 554 us -> 432 us (0.78)
  blocking collectives: 183 us -> 60.9 us
    psum x1 -> x2, blocking collectives: 183 us -> 60.9 us  [local(): traces = lax.psum(lax.psum(jnp.stack(recorded, axis=-1), 'gy'), 'gx')]
  transfers between devices with their start and end apart: 33 -> 33, of which waited for: 17 -> 17; matrix products, arithmetic and copies ran while one was open for 29% -> 37% of each run, Pallas kernels for 0% -> 0%
where the time goes in v1:
time: 432 us; the launch traced here: 430 us
  local copies, waits for them, and re-layouts  177 us (41%)
  starting transfers between devices  113 us (26%)
  blocking collectives  60.9 us (14%)
  waiting for transfers between devices  39.1 us (9%)
  other arithmetic  24.3 us (6%)
  between operations  16 us (4%)
    div x8, local copies, waits for them, and re-layouts, advance(): (2.0 * middle - (1.0 - damp) * previous + coef * laplace(extended) + inje...  133 us
    ppermute x16, starting transfers between devices, extended_2(): lax.ppermute(tail, axis, [(i, (i + 1) % count) for i in range(ends)])  92.4 us
    psum x2, blocking collectives, local(): traces = lax.psum(lax.psum(jnp.stack(recorded, axis=-1), 'gy'), 'gx')  60.9 us
    all_gather x1, waiting for transfers between devices, local(): piece = lax.all_gather(model_tiles, ('shot', 'gx'), axis=0, tiled=True)  24.6 us
    gather x8, local copies, waits for them, and re-layouts, sample(): field[:, jnp.clip(local_x, 0, size_x - 1), jnp.clip(local_y, 0, size_y -...  23.6 us
    ppermute x16, starting transfers between devices, extended_2(): lax.ppermute(head, axis, [((i + 1) % count, i) for i in range(ends)])  20.7 us
    div x8, other arithmetic, advance(): (2.0 * middle - (1.0 - damp) * previous + coef * laplace(extended) + inje...  16.9 us
    slice x16, local copies, waits for them, and re-layouts, depth_ahead(): return jnp.concatenate([field[..., reach:], filler], axis=-1)  12.5 us
  transfers between devices with their start and end apart: 33, of which 17 were waited for; matrix products, arithmetic and copies ran while one was open for 37% of the time, Pallas kernels for 0%

profile of v1, /device:TPU:0, one launch (start us, length us, event | category | flops | bytes accessed | tf_op | source)
XLA Modules:
  0.0 430.3 jit_solution(1766614489517195570)
XLA Ops:
  28.2 6.1 %collective-permute-start.3 = (f32[2,20,2,128]{3,2,1,0:T(2,128)S(1)}, f32[2,20,2,128]{3,2,1,0:T(2,128)S(1)}, u32[]{:S(2)}, u32[]{:S(2)}) collective-permute-start(f32[2,20,2,128]{3,2,1,0:T(2,128)S(1)} %get-tuple-element.57), channel_id=1, source_target_pairs={{0,1},{1,2},{2,3},{3,4},{4,5},{5,6},{6,7},{8,9},{9,10},{10,11},{11... | collective-permute-start | bytes 122888 | tf_op jit(solution)/shard_map/ppermute | solution.py:21
  37.5 24.6 %all-gather.2.cloned.1.call-done = f32[256,32,128]{2,1,0:T(8,128)} async-done(((f32[16,32,128]{2,1,0:T(8,128)}), f32[256,32,128]{2,1,0:T(8,128)}) %all-gather.2.cloned.1.call-update) | async-done | bytes 4194320 | tf_op jit(solution)/shard_map/all_gather | solution.py:113
  77.4 6.1 %collective-permute-start.7 = (f32[2,20,2,128]{3,2,1,0:T(2,128)S(1)}, f32[2,20,2,128]{3,2,1,0:T(2,128)S(1)}, u32[]{:S(2)}, u32[]{:S(2)}) collective-permute-start(f32[2,20,2,128]{3,2,1,0:T(2,128)S(1)} %get-tuple-element.53), channel_id=1, source_target_pairs={{0,1},{1,2},{2,3},{3,4},{4,5},{5,6},{6,7},{8,9},{9,10},{10,11},{11... | collective-permute-start | bytes 122888 | tf_op jit(solution)/shard_map/ppermute | solution.py:21
  84.4 16.6 %copy.515 = f32[2,16,32,128]{0,3,2,1:T(8,128)} copy(f32[2,16,32,128]{3,2,1,0:T(8,128)S(1)} %fusion.94) | data formatting | bytes 1048576 | tf_op jit(solution)/shard_map/div | solution.py:86
  107.5 5.0 %collective-permute-start.9 = (f32[2,2,32,128]{3,2,1,0:T(8,128)S(1)}, f32[2,2,32,128]{3,2,1,0:T(8,128)S(1)}, u32[]{:S(2)}, u32[]{:S(2)}) collective-permute-start(f32[2,2,32,128]{3,2,1,0:T(8,128)S(1)} %get-tuple-element.93), channel_id=1, source_target_pairs={{0,8},{8,16},{16,24},{1,9},{9,17},{17,25},{2,10},{10,18},{18,26},{... | collective-permute-start | bytes 196616 | tf_op jit(solution)/shard_map/ppermute | solution.py:21
  115.8 6.5 %collective-permute-start.11 = (f32[2,20,2,128]{3,2,1,0:T(2,128)S(1)}, f32[2,20,2,128]{3,2,1,0:T(2,128)S(1)}, u32[]{:S(2)}, u32[]{:S(2)}) collective-permute-start(f32[2,20,2,128]{3,2,1,0:T(2,128)S(1)} %get-tuple-element.49), channel_id=1, source_target_pairs={{0,1},{1,2},{2,3},{3,4},{4,5},{5,6},{6,7},{8,9},{9,10},{10,11},{11... | collective-permute-start | bytes 122888 | tf_op jit(solution)/shard_map/ppermute | solution.py:21
  123.3 16.6 %copy.516 = f32[2,16,32,128]{0,3,2,1:T(8,128)} copy(f32[2,16,32,128]{3,2,1,0:T(8,128)S(1)} %fusion.82) | data formatting | bytes 1048576 | tf_op jit(solution)/shard_map/div | solution.py:86
  146.4 4.9 %collective-permute-start.13 = (f32[2,2,32,128]{3,2,1,0:T(8,128)S(1)}, f32[2,2,32,128]{3,2,1,0:T(8,128)S(1)}, u32[]{:S(2)}, u32[]{:S(2)}) collective-permute-start(f32[2,2,32,128]{3,2,1,0:T(8,128)S(1)} %get-tuple-element.87), channel_id=1, source_target_pairs={{0,8},{8,16},{16,24},{1,9},{9,17},{17,25},{2,10},{10,18},{18,26},{... | collective-permute-start | bytes 196616 | tf_op jit(solution)/shard_map/ppermute | solution.py:21
  154.5 7.0 %collective-permute-start.15 = (f32[2,20,2,128]{3,2,1,0:T(2,128)S(1)}, f32[2,20,2,128]{3,2,1,0:T(2,128)S(1)}, u32[]{:S(2)}, u32[]{:S(2)}) collective-permute-start(f32[2,20,2,128]{3,2,1,0:T(2,128)S(1)} %get-tuple-element.45), channel_id=1, source_target_pairs={{0,1},{1,2},{2,3},{3,4},{4,5},{5,6},{6,7},{8,9},{9,10},{10,11},{11... | collective-permute-start | bytes 122888 | tf_op jit(solution)/shard_map/ppermute | solution.py:21
  162.4 16.6 %copy.517 = f32[2,16,32,128]{0,3,2,1:T(8,128)} copy(f32[2,16,32,128]{3,2,1,0:T(8,128)S(1)} %fusion.70) | data formatting | bytes 1048576 | tf_op jit(solution)/shard_map/div | solution.py:86
  185.6 4.9 %collective-permute-start.17 = (f32[2,2,32,128]{3,2,1,0:T(8,128)S(1)}, f32[2,2,32,128]{3,2,1,0:T(8,128)S(1)}, u32[]{:S(2)}, u32[]{:S(2)}) collective-permute-start(f32[2,2,32,128]{3,2,1,0:T(8,128)S(1)} %get-tuple-element.81), channel_id=1, source_target_pairs={{0,8},{8,16},{16,24},{1,9},{9,17},{17,25},{2,10},{10,18},{18,26},{... | collective-permute-start | bytes 196616 | tf_op jit(solution)/shard_map/ppermute | solution.py:21
  193.7 7.1 %collective-permute-start.19 = (f32[2,20,2,128]{3,2,1,0:T(2,128)S(1)}, f32[2,20,2,128]{3,2,1,0:T(2,128)S(1)}, u32[]{:S(2)}, u32[]{:S(2)}) collective-permute-start(f32[2,20,2,128]{3,2,1,0:T(2,128)S(1)} %get-tuple-element.41), channel_id=1, source_target_pairs={{0,1},{1,2},{2,3},{3,4},{4,5},{5,6},{6,7},{8,9},{9,10},{10,11},{11... | collective-permute-start | bytes 122888 | tf_op jit(solution)/shard_map/ppermute | solution.py:21
  201.8 16.6 %copy.518 = f32[2,16,32,128]{0,3,2,1:T(8,128)} copy(f32[2,16,32,128]{3,2,1,0:T(8,128)S(1)} %fusion.58) | data formatting | bytes 1048576 | tf_op jit(solution)/shard_map/div | solution.py:86
  224.9 4.9 %collective-permute-start.21 = (f32[2,2,32,128]{3,2,1,0:T(8,128)S(1)}, f32[2,2,32,128]{3,2,1,0:T(8,128)S(1)}, u32[]{:S(2)}, u32[]{:S(2)}) collective-permute-start(f32[2,2,32,128]{3,2,1,0:T(8,128)S(1)} %get-tuple-element.75), channel_id=1, source_target_pairs={{0,8},{8,16},{16,24},{1,9},{9,17},{17,25},{2,10},{10,18},{18,26},{... | collective-permute-start | bytes 196616 | tf_op jit(solution)/shard_map/ppermute | solution.py:21
  233.0 7.0 %collective-permute-start.23 = (f32[2,20,2,128]{3,2,1,0:T(2,128)S(1)}, f32[2,20,2,128]{3,2,1,0:T(2,128)S(1)}, u32[]{:S(2)}, u32[]{:S(2)}) collective-permute-start(f32[2,20,2,128]{3,2,1,0:T(2,128)S(1)} %get-tuple-element.37), channel_id=1, source_target_pairs={{0,1},{1,2},{2,3},{3,4},{4,5},{5,6},{6,7},{8,9},{9,10},{10,11},{11... | collective-permute-start | bytes 122888 | tf_op jit(solution)/shard_map/ppermute | solution.py:21
  240.9 16.6 %copy.519 = f32[2,16,32,128]{0,3,2,1:T(8,128)} copy(f32[2,16,32,128]{3,2,1,0:T(8,128)S(1)} %fusion.46) | data formatting | bytes 1048576 | tf_op jit(solution)/shard_map/div | solution.py:86
  264.1 4.9 %collective-permute-start.25 = (f32[2,2,32,128]{3,2,1,0:T(8,128)S(1)}, f32[2,2,32,128]{3,2,1,0:T(8,128)S(1)}, u32[]{:S(2)}, u32[]{:S(2)}) collective-permute-start(f32[2,2,32,128]{3,2,1,0:T(8,128)S(1)} %get-tuple-element.69), channel_id=1, source_target_pairs={{0,8},{8,16},{16,24},{1,9},{9,17},{17,25},{2,10},{10,18},{18,26},{... | collective-permute-start | bytes 196616 | tf_op jit(solution)/shard_map/ppermute | solution.py:21
  272.2 7.0 %collective-permute-start.27 = (f32[2,20,2,128]{3,2,1,0:T(2,128)S(1)}, f32[2,20,2,128]{3,2,1,0:T(2,128)S(1)}, u32[]{:S(2)}, u32[]{:S(2)}) collective-permute-start(f32[2,20,2,128]{3,2,1,0:T(2,128)S(1)} %get-tuple-element.33), channel_id=1, source_target_pairs={{0,1},{1,2},{2,3},{3,4},{4,5},{5,6},{6,7},{8,9},{9,10},{10,11},{11... | collective-permute-start | bytes 122888 | tf_op jit(solution)/shard_map/ppermute | solution.py:21
  280.1 16.6 %copy.520 = f32[2,16,32,128]{0,3,2,1:T(8,128)} copy(f32[2,16,32,128]{3,2,1,0:T(8,128)S(1)} %fusion.34) | data formatting | bytes 1048576 | tf_op jit(solution)/shard_map/div | solution.py:86
  311.4 7.2 %collective-permute-start.31 = (f32[2,20,2,128]{3,2,1,0:T(2,128)S(1)}, f32[2,20,2,128]{3,2,1,0:T(2,128)S(1)}, u32[]{:S(2)}, u32[]{:S(2)}) collective-permute-start(f32[2,20,2,128]{3,2,1,0:T(2,128)S(1)} %get-tuple-element.29), channel_id=1, source_target_pairs={{0,1},{1,2},{2,3},{3,4},{4,5},{5,6},{6,7},{8,9},{9,10},{10,11},{11... | collective-permute-start | bytes 122888 | tf_op jit(solution)/shard_map/ppermute | solution.py:21
  319.5 16.6 %copy.521 = f32[2,16,32,128]{0,3,2,1:T(8,128)} copy(f32[2,16,32,128]{3,2,1,0:T(8,128)S(1)} %fusion.22) | data formatting | bytes 1048576 | tf_op jit(solution)/shard_map/div | solution.py:86
  341.4 16.7 %copy.522 = f32[2,16,32,128]{0,3,2,1:T(8,128)} copy(f32[2,16,32,128]{3,2,1,0:T(8,128)S(1)} %fusion.10) | data formatting | bytes 1048576 | tf_op jit(solution)/shard_map/div | solution.py:86
  362.6 41.2 %psum.14 = f32[2,256,8]{1,2,0:T(8,128)S(1)} all-reduce(f32[2,256,8]{1,2,0:T(8,128)S(1)} %stack.2), channel_id=1, replica_groups=mesh['shot'=4,'gx'=4,'gy'=8] {'gy'}, use_global_device_ids=true, to_apply=%region_1.2 | all-reduce | flops 4096 | bytes 32768 | tf_op jit(solution)/shard_map/psum | solution.py:138
  403.8 19.7 %psum.15 = f32[1,2,256,8]{2,3,1,0:T(8,128)} all-reduce(f32[1,2,256,8]{2,3,1,0:T(8,128)S(1)} %bitcast.70), channel_id=1, replica_groups=mesh['shot'=4,'gx'=4,'gy'=8] {'gx'}, use_global_device_ids=true, to_apply=%region_2.3 | all-reduce | flops 4096 | bytes 32768 | tf_op jit(solution)/shard_map/psum | solution.py:138
  (165 shorter events, 117.2 us)
Async XLA Ops:
  7.2 54.9 %all-gather.2.cloned.1.call-start = ((), (), s32[]{:S(2)}) async-start(), calls=%async_computation | async-start | bytes 4456448 | tf_op jit(solution)/shard_map/all_gather | solution.py:113
  8.8 17.0 %collective-permute-start = (f32[2,2,32,128]{3,2,1,0:T(8,128)S(1)}, f32[2,2,32,128]{3,2,1,0:T(8,128)S(1)}, u32[]{:S(2)}, u32[]{:S(2)}) collective-permute-start(f32[2,2,32,128]{3,2,1,0:T(8,128)S(1)} %get-tuple-element.104), channel_id=1, source_target_pairs={{8,0},{16,8},{24,16},{9,1},{17,9},{25,17},{10,2},{18,10},{26,18},{... | collective-permute-start | bytes 196616 | tf_op jit(solution)/shard_map/ppermute | solution.py:23
  10.1 15.8 %collective-permute-start.1 = (f32[2,2,32,128]{3,2,1,0:T(8,128)S(1)}, f32[2,2,32,128]{3,2,1,0:T(8,128)S(1)}, u32[]{:S(2)}, u32[]{:S(2)}) collective-permute-start(f32[2,2,32,128]{3,2,1,0:T(8,128)S(1)} %get-tuple-element.105), channel_id=1, source_target_pairs={{0,8},{8,16},{16,24},{1,9},{9,17},{17,25},{2,10},{10,18},{18,26},{... | collective-permute-start | bytes 196616 | tf_op jit(solution)/shard_map/ppermute | solution.py:21
  26.9 7.7 %collective-permute-start.2 = (f32[2,20,2,128]{3,2,1,0:T(2,128)S(1)}, f32[2,20,2,128]{3,2,1,0:T(2,128)S(1)}, u32[]{:S(2)}, u32[]{:S(2)}) collective-permute-start(f32[2,20,2,128]{3,2,1,0:T(2,128)S(1)} %get-tuple-element.56), channel_id=1, source_target_pairs={{1,0},{2,1},{3,2},{4,3},{5,4},{6,5},{7,6},{9,8},{10,9},{11,10},{12... | collective-permute-start | bytes 122888 | tf_op jit(solution)/shard_map/ppermute | solution.py:23
  28.2 7.9 %collective-permute-start.3 = (f32[2,20,2,128]{3,2,1,0:T(2,128)S(1)}, f32[2,20,2,128]{3,2,1,0:T(2,128)S(1)}, u32[]{:S(2)}, u32[]{:S(2)}) collective-permute-start(f32[2,20,2,128]{3,2,1,0:T(2,128)S(1)} %get-tuple-element.57), channel_id=1, source_target_pairs={{0,1},{1,2},{2,3},{3,4},{4,5},{5,6},{6,7},{8,9},{9,10},{10,11},{11... | collective-permute-start | bytes 122888 | tf_op jit(solution)/shard_map/ppermute | solution.py:21
  76.1 28.0 %collective-permute-start.6 = (f32[2,20,2,128]{3,2,1,0:T(2,128)S(1)}, f32[2,20,2,128]{3,2,1,0:T(2,128)S(1)}, u32[]{:S(2)}, u32[]{:S(2)}) collective-permute-start(f32[2,20,2,128]{3,2,1,0:T(2,128)S(1)} %get-tuple-element.52), channel_id=1, source_target_pairs={{1,0},{2,1},{3,2},{4,3},{5,4},{6,5},{7,6},{9,8},{10,9},{11,10},{12... | collective-permute-start | bytes 122888 | tf_op jit(solution)/shard_map/ppermute | solution.py:23
  77.4 26.7 %collective-permute-start.7 = (f32[2,20,2,128]{3,2,1,0:T(2,128)S(1)}, f32[2,20,2,128]{3,2,1,0:T(2,128)S(1)}, u32[]{:S(2)}, u32[]{:S(2)}) collective-permute-start(f32[2,20,2,128]{3,2,1,0:T(2,128)S(1)} %get-tuple-element.53), channel_id=1, source_target_pairs={{0,1},{1,2},{2,3},{3,4},{4,5},{5,6},{6,7},{8,9},{9,10},{10,11},{11... | collective-permute-start | bytes 122888 | tf_op jit(solution)/shard_map/ppermute | solution.py:21
  107.5 6.9 %collective-permute-start.9 = (f32[2,2,32,128]{3,2,1,0:T(8,128)S(1)}, f32[2,2,32,128]{3,2,1,0:T(8,128)S(1)}, u32[]{:S(2)}, u32[]{:S(2)}) collective-permute-start(f32[2,2,32,128]{3,2,1,0:T(8,128)S(1)} %get-tuple-element.93), channel_id=1, source_target_pairs={{0,8},{8,16},{16,24},{1,9},{9,17},{17,25},{2,10},{10,18},{18,26},{... | collective-permute-start | bytes 196616 | tf_op jit(solution)/shard_map/ppermute | solution.py:21
  114.5 28.4 %collective-permute-start.10 = (f32[2,20,2,128]{3,2,1,0:T(2,128)S(1)}, f32[2,20,2,128]{3,2,1,0:T(2,128)S(1)}, u32[]{:S(2)}, u32[]{:S(2)}) collective-permute-start(f32[2,20,2,128]{3,2,1,0:T(2,128)S(1)} %get-tuple-element.48), channel_id=1, source_target_pairs={{1,0},{2,1},{3,2},{4,3},{5,4},{6,5},{7,6},{9,8},{10,9},{11,10},{12... | collective-permute-start | bytes 122888 | tf_op jit(solution)/shard_map/ppermute | solution.py:23
  115.8 27.1 %collective-permute-start.11 = (f32[2,20,2,128]{3,2,1,0:T(2,128)S(1)}, f32[2,20,2,128]{3,2,1,0:T(2,128)S(1)}, u32[]{:S(2)}, u32[]{:S(2)}) collective-permute-start(f32[2,20,2,128]{3,2,1,0:T(2,128)S(1)} %get-tuple-element.49), channel_id=1, source_target_pairs={{0,1},{1,2},{2,3},{3,4},{4,5},{5,6},{6,7},{8,9},{9,10},{10,11},{11... | collective-permute-start | bytes 122888 | tf_op jit(solution)/shard_map/ppermute | solution.py:21
  153.2 28.9 %collective-permute-start.14 = (f32[2,20,2,128]{3,2,1,0:T(2,128)S(1)}, f32[2,20,2,128]{3,2,1,0:T(2,128)S(1)}, u32[]{:S(2)}, u32[]{:S(2)}) collective-permute-start(f32[2,20,2,128]{3,2,1,0:T(2,128)S(1)} %get-tuple-element.44), channel_id=1, source_target_pairs={{1,0},{2,1},{3,2},{4,3},{5,4},{6,5},{7,6},{9,8},{10,9},{11,10},{12... | collective-permute-start | bytes 122888 | tf_op jit(solution)/shard_map/ppermute | solution.py:23
  154.5 27.6 %collective-permute-start.15 = (f32[2,20,2,128]{3,2,1,0:T(2,128)S(1)}, f32[2,20,2,128]{3,2,1,0:T(2,128)S(1)}, u32[]{:S(2)}, u32[]{:S(2)}) collective-permute-start(f32[2,20,2,128]{3,2,1,0:T(2,128)S(1)} %get-tuple-element.45), channel_id=1, source_target_pairs={{0,1},{1,2},{2,3},{3,4},{4,5},{5,6},{6,7},{8,9},{9,10},{10,11},{11... | collective-permute-start | bytes 122888 | tf_op jit(solution)/shard_map/ppermute | solution.py:21
  185.6 6.8 %collective-permute-start.17 = (f32[2,2,32,128]{3,2,1,0:T(8,128)S(1)}, f32[2,2,32,128]{3,2,1,0:T(8,128)S(1)}, u32[]{:S(2)}, u32[]{:S(2)}) collective-permute-start(f32[2,2,32,128]{3,2,1,0:T(8,128)S(1)} %get-tuple-element.81), channel_id=1, source_target_pairs={{0,8},{8,16},{16,24},{1,9},{9,17},{17,25},{2,10},{10,18},{18,26},{... | collective-permute-start | bytes 196616 | tf_op jit(solution)/shard_map/ppermute | solution.py:21
  192.4 29.1 %collective-permute-start.18 = (f32[2,20,2,128]{3,2,1,0:T(2,128)S(1)}, f32[2,20,2,128]{3,2,1,0:T(2,128)S(1)}, u32[]{:S(2)}, u32[]{:S(2)}) collective-permute-start(f32[2,20,2,128]{3,2,1,0:T(2,128)S(1)} %get-tuple-element.40), channel_id=1, source_target_pairs={{1,0},{2,1},{3,2},{4,3},{5,4},{6,5},{7,6},{9,8},{10,9},{11,10},{12... | collective-permute-start | bytes 122888 | tf_op jit(solution)/shard_map/ppermute | solution.py:23
  193.7 27.8 %collective-permute-start.19 = (f32[2,20,2,128]{3,2,1,0:T(2,128)S(1)}, f32[2,20,2,128]{3,2,1,0:T(2,128)S(1)}, u32[]{:S(2)}, u32[]{:S(2)}) collective-permute-start(f32[2,20,2,128]{3,2,1,0:T(2,128)S(1)} %get-tuple-element.41), channel_id=1, source_target_pairs={{0,1},{1,2},{2,3},{3,4},{4,5},{5,6},{6,7},{8,9},{9,10},{10,11},{11... | collective-permute-start | bytes 122888 | tf_op jit(solution)/shard_map/ppermute | solution.py:21
  224.9 6.8 %collective-permute-start.21 = (f32[2,2,32,128]{3,2,1,0:T(8,128)S(1)}, f32[2,2,32,128]{3,2,1,0:T(8,128)S(1)}, u32[]{:S(2)}, u32[]{:S(2)}) collective-permute-start(f32[2,2,32,128]{3,2,1,0:T(8,128)S(1)} %get-tuple-element.75), channel_id=1, source_target_pairs={{0,8},{8,16},{16,24},{1,9},{9,17},{17,25},{2,10},{10,18},{18,26},{... | collective-permute-start | bytes 196616 | tf_op jit(solution)/shard_map/ppermute | solution.py:21
  231.7 28.9 %collective-permute-start.22 = (f32[2,20,2,128]{3,2,1,0:T(2,128)S(1)}, f32[2,20,2,128]{3,2,1,0:T(2,128)S(1)}, u32[]{:S(2)}, u32[]{:S(2)}) collective-permute-start(f32[2,20,2,128]{3,2,1,0:T(2,128)S(1)} %get-tuple-element.36), channel_id=1, source_target_pairs={{1,0},{2,1},{3,2},{4,3},{5,4},{6,5},{7,6},{9,8},{10,9},{11,10},{12... | collective-permute-start | bytes 122888 | tf_op jit(solution)/shard_map/ppermute | solution.py:23
  233.0 27.6 %collective-permute-start.23 = (f32[2,20,2,128]{3,2,1,0:T(2,128)S(1)}, f32[2,20,2,128]{3,2,1,0:T(2,128)S(1)}, u32[]{:S(2)}, u32[]{:S(2)}) collective-permute-start(f32[2,20,2,128]{3,2,1,0:T(2,128)S(1)} %get-tuple-element.37), channel_id=1, source_target_pairs={{0,1},{1,2},{2,3},{3,4},{4,5},{5,6},{6,7},{8,9},{9,10},{10,11},{11... | collective-permute-start | bytes 122888 | tf_op jit(solution)/shard_map/ppermute | solution.py:21
  264.1 6.8 %collective-permute-start.25 = (f32[2,2,32,128]{3,2,1,0:T(8,128)S(1)}, f32[2,2,32,128]{3,2,1,0:T(8,128)S(1)}, u32[]{:S(2)}, u32[]{:S(2)}) collective-permute-start(f32[2,2,32,128]{3,2,1,0:T(8,128)S(1)} %get-tuple-element.69), channel_id=1, source_target_pairs={{0,8},{8,16},{16,24},{1,9},{9,17},{17,25},{2,10},{10,18},{18,26},{... | collective-permute-start | bytes 196616 | tf_op jit(solution)/shard_map/ppermute | solution.py:21
  270.9 28.9 %collective-permute-start.26 = (f32[2,20,2,128]{3,2,1,0:T(2,128)S(1)}, f32[2,20,2,128]{3,2,1,0:T(2,128)S(1)}, u32[]{:S(2)}, u32[]{:S(2)}) collective-permute-start(f32[2,20,2,128]{3,2,1,0:T(2,128)S(1)} %get-tuple-element.32), channel_id=1, source_target_pairs={{1,0},{2,1},{3,2},{4,3},{5,4},{6,5},{7,6},{9,8},{10,9},{11,10},{12... | collective-permute-start | bytes 122888 | tf_op jit(solution)/shard_map/ppermute | solution.py:23
  272.2 27.6 %collective-permute-start.27 = (f32[2,20,2,128]{3,2,1,0:T(2,128)S(1)}, f32[2,20,2,128]{3,2,1,0:T(2,128)S(1)}, u32[]{:S(2)}, u32[]{:S(2)}) collective-permute-start(f32[2,20,2,128]{3,2,1,0:T(2,128)S(1)} %get-tuple-element.33), channel_id=1, source_target_pairs={{0,1},{1,2},{2,3},{3,4},{4,5},{5,6},{6,7},{8,9},{9,10},{10,11},{11... | collective-permute-start | bytes 122888 | tf_op jit(solution)/shard_map/ppermute | solution.py:21
  303.3 6.8 %collective-permute-start.29 = (f32[2,2,32,128]{3,2,1,0:T(8,128)S(1)}, f32[2,2,32,128]{3,2,1,0:T(8,128)S(1)}, u32[]{:S(2)}, u32[]{:S(2)}) collective-permute-start(f32[2,2,32,128]{3,2,1,0:T(8,128)S(1)} %get-tuple-element.63), channel_id=1, source_target_pairs={{0,8},{8,16},{16,24},{1,9},{9,17},{17,25},{2,10},{10,18},{18,26},{... | collective-permute-start | bytes 196616 | tf_op jit(solution)/shard_map/ppermute | solution.py:21
  310.1 29.1 %collective-permute-start.30 = (f32[2,20,2,128]{3,2,1,0:T(2,128)S(1)}, f32[2,20,2,128]{3,2,1,0:T(2,128)S(1)}, u32[]{:S(2)}, u32[]{:S(2)}) collective-permute-start(f32[2,20,2,128]{3,2,1,0:T(2,128)S(1)} %get-tuple-element.28), channel_id=1, source_target_pairs={{1,0},{2,1},{3,2},{4,3},{5,4},{6,5},{7,6},{9,8},{10,9},{11,10},{12... | collective-permute-start | bytes 122888 | tf_op jit(solution)/shard_map/ppermute | solution.py:23
  311.4 27.8 %collective-permute-start.31 = (f32[2,20,2,128]{3,2,1,0:T(2,128)S(1)}, f32[2,20,2,128]{3,2,1,0:T(2,128)S(1)}, u32[]{:S(2)}, u32[]{:S(2)}) collective-permute-start(f32[2,20,2,128]{3,2,1,0:T(2,128)S(1)} %get-tuple-element.29), channel_id=1, source_target_pairs={{0,1},{1,2},{2,3},{3,4},{4,5},{5,6},{6,7},{8,9},{9,10},{10,11},{11... | collective-permute-start | bytes 122888 | tf_op jit(solution)/shard_map/ppermute | solution.py:21
  (22 other events, 594.3 us)
Sparse Core Ops, SparseCore 0:
  9.7 52.3 all-gather.1
